TPU v7x, 32 devices: a whole 2x2x4 slice. The times are simulated.
32 devices in a mesh: ctx: 4 (over y, x), exp: 8 (over z, core).
Axes of the slice: x: 2, y: 2, z: 4, core: 2. Of those that a mesh axis runs over, the one named last changes fastest.
Arguments:
- residual: bfloat16 [512, 4096], P('ctx'), may hold values from -4 to 4
- ssm_input: bfloat16 [512, 8192], P('ctx', 'exp'), may hold values from -16 to 16
- ssm_gate: bfloat16 [512, 8192], P('ctx', 'exp'), may hold values from -5 to 5
- write_vectors: bfloat16 [512, 128], P('ctx'), may hold values from -1.75 to 1.75
- read_vectors: bfloat16 [512, 128], P('ctx'), may hold values from -1.75 to 1.75
- step_logits: float32 [128, 512], P('exp', 'ctx'), may hold values from -2 to 1536
- decay_log: float32 [128], P('exp'), may hold values from -12 to -2
- skip_gain: float32 [128], P('exp'), may hold values from 0.5 to 3
- norm_gain: float32 [8192], P('exp'), may hold values from 0.1 to 1.9
- out_weight: bfloat16 [8192, 4096], P('exp', 'ctx'), may hold values from -0.09375 to 0.09375
- moe_gain: float32 [4096], replicated, may hold values from 0.1 to 1.9
- gate_weight: bfloat16 [8, 4096, 12288], P('exp', None, 'ctx'), may hold values from -0.09375 to 0.09375
- up_weight: bfloat16 [8, 4096, 12288], P('exp', None, 'ctx'), may hold values from -0.09375 to 0.09375
- down_weight: bfloat16 [8, 12288, 4096], P('exp', 'ctx'), may hold values from -0.0546875 to 0.0546875
- expert_ids: int32 [512, 2], P('ctx'), may hold values from 0 to 7, all different within a row; in each aligned block of 128 rows (0 to 127, 128 to 255, ...) at most 64 rows name the same one
- route_weight: float32 [512, 2], P('ctx'), may hold values from 0.5 to 1.5
Outputs:
- layer_out: bfloat16 [512, 4096], P('ctx', 'exp')
Inputs may be any that keep to these rules, and one draw needn't show every extreme that they name: `expert_ids`: each row names 2 different experts. Among the 128 rows of one index of ctx no expert is named by more than 64 rows, and in every draw some expert is named by exactly 64 of them.
All inputs are finite; a program needn't handle non-finite values.
Results may differ from a plain program's by a relative error of at most 0.023.
Values may be sent and summed in bfloat16 or wider, within the bound.
A program may use at most 192 MiB of HBM per device.

v0:
```python
import jax
import jax.numpy as jnp
from jax import lax
from jax.sharding import PartitionSpec as P

SPAN = 128
NORM_GROUP = 512
EXPERTS = 8
CAP = 64
EPSILON = 1e-05


def passed_along(block, axis, distance):
    devices = range(lax.axis_size(axis))
    route = [(i - distance, i) for i in devices if i - distance in devices]
    return lax.ppermute(block, axis, route)


def slot_tables(block_ids):
    expert_range = jnp.arange(EXPERTS, dtype=jnp.int32)
    hit_table = jnp.sum(
        (block_ids[:, :, None] == expert_range[None, None, :]).astype(jnp.int32), axis=1
    )
    ranking = jnp.cumsum(hit_table, axis=0) - 1
    slot_range = jnp.arange(CAP, dtype=jnp.int32)
    matches = (hit_table.T[:, None, :] == 1) & (ranking.T[:, None, :] == slot_range[None, :, None])
    row_count = block_ids.shape[0]
    row_range = jnp.arange(row_count, dtype=jnp.int32)
    chosen = jnp.sum(jnp.where(matches, row_range[None, None, :], 0), axis=2)
    filled = jnp.any(matches, axis=2)
    token_of_slot = jnp.where(filled, chosen, row_count)
    pick_rank = jnp.take_along_axis(ranking, block_ids, axis=1)
    return (token_of_slot, pick_rank)


def normalize(stream_rows, moe_gain):
    values = stream_rows.astype(jnp.float32)
    scale_inv = lax.rsqrt(jnp.mean(values * values, axis=-1, keepdims=True) + EPSILON)
    return (values * scale_inv * moe_gain).astype(jnp.bfloat16)


def body(
    residual,
    ssm_input,
    ssm_gate,
    write_vectors,
    read_vectors,
    step_logits,
    decay_log,
    skip_gain,
    norm_gain,
    out_weight,
    moe_gain,
    gate_weight,
    up_weight,
    down_weight,
    expert_ids,
    route_weight,
):
    heads_dev = step_logits.shape[0]
    tok_rows = step_logits.shape[1]
    head_width = ssm_input.shape[1] // heads_dev
    span_count = tok_rows // SPAN
    step_size = jax.nn.softplus(step_logits)
    log_step = step_size * (-jnp.exp(decay_log))[:, None]
    cumulative = jnp.cumsum(log_step.reshape(heads_dev, span_count, SPAN), axis=2)
    step_blocks = step_size.reshape(heads_dev, span_count, SPAN)
    input_blocks = ssm_input.reshape(span_count, SPAN, heads_dev, head_width)
    write_blocks = write_vectors.reshape(span_count, SPAN, -1)
    read_blocks = read_vectors.reshape(span_count, SPAN, -1)
    scores = jnp.einsum(
        "ktn,ksn->kts", read_blocks, write_blocks, preferred_element_type=jnp.float32
    )
    causal = jnp.arange(SPAN)[:, None] >= jnp.arange(SPAN)[None, :]
    log_gaps = cumulative[:, :, :, None] - cumulative[:, :, None, :]
    mixing = jnp.where(
        causal,
        scores[None] * jnp.exp(jnp.where(causal, log_gaps, 0.0)) * step_blocks[:, :, None, :],
        0.0,
    ).astype(jnp.bfloat16)
    intra_out = jnp.einsum(
        "hkts,kshp->kthp", mixing, input_blocks, preferred_element_type=jnp.float32
    )
    end_weight = jnp.exp(cumulative[:, :, -1:] - cumulative) * step_blocks
    loaded = (end_weight[:, :, :, None] * write_blocks.astype(jnp.float32)[None]).astype(
        jnp.bfloat16
    )
    block_state = jnp.einsum(
        "kshp,hksn->hkpn", input_blocks, loaded, preferred_element_type=jnp.float32
    )
    block_decay = jnp.exp(cumulative[:, :, -1])
    running = jnp.zeros_like(block_state[:, 0])
    decay_run = jnp.ones_like(block_decay[:, 0])
    entering_list = [running]
    reach_list = [decay_run]
    running = block_decay[:, 0, None, None] * running + block_state[:, 0]
    decay_run = decay_run * block_decay[:, 0]
    device_state = running
    device_decay = decay_run

    def forward(turn_index, incoming):
        return passed_along(
            (device_decay[:, None, None] * incoming + device_state).astype(jnp.bfloat16), "ctx", 1
        ).astype(jnp.float32)

    device_in = lax.fori_loop(0, lax.axis_size("ctx") - 1, forward, jnp.zeros_like(device_state))
    entering = jnp.stack(entering_list, axis=1)
    reach = jnp.stack(reach_list, axis=1)
    states = entering + reach[:, :, None, None] * device_in[:, None]
    inter_out = jnp.transpose(jnp.exp(cumulative), (1, 2, 0))[:, :, :, None] * jnp.einsum(
        "ktn,hkpn->kthp", read_blocks.astype(jnp.float32), states, precision=lax.Precision.HIGHEST
    )
    scan_out = (
        intra_out + inter_out + skip_gain[None, None, :, None] * input_blocks.astype(jnp.float32)
    )
    scan_out = scan_out.reshape(tok_rows, heads_dev * head_width)
    gated_out = scan_out * jax.nn.silu(ssm_gate.astype(jnp.float32))
    grouped = gated_out.reshape(tok_rows, -1, NORM_GROUP)
    group_scale = lax.rsqrt(jnp.mean(grouped * grouped, axis=2, keepdims=True) + EPSILON)
    normed = ((grouped * group_scale).reshape(tok_rows, -1) * norm_gain).astype(jnp.bfloat16)
    ssm_terms = jnp.dot(
        normed,
        lax.all_gather(out_weight, "ctx", axis=1, tiled=True),
        preferred_element_type=jnp.float32,
    )
    exp_count = lax.axis_size("exp")
    exp_index = lax.axis_index("exp")
    slice_width = residual.shape[1] // exp_count
    split_count = exp_count // EXPERTS
    own_residual = lax.dynamic_slice_in_dim(residual, exp_index * slice_width, slice_width, 1)
    ssm_sum = lax.psum(ssm_terms.astype(jnp.bfloat16), "exp").astype(jnp.float32)
    ssm_share = lax.dynamic_slice_in_dim(ssm_sum, exp_index * slice_width, slice_width, 1)
    stream_slice = (own_residual.astype(jnp.float32) + ssm_share).astype(jnp.bfloat16)
    token_of_slot, pick_rank = slot_tables(expert_ids)
    stream_full = lax.all_gather(stream_slice, "exp", axis=1, tiled=True)
    padded = jnp.concatenate(
        [stream_full, jnp.zeros((1, stream_full.shape[1]), jnp.bfloat16)], axis=0
    )
    my_slots = lax.dynamic_index_in_dim(token_of_slot, exp_index // split_count, 0, keepdims=False)
    picked = normalize(jnp.take(padded, my_slots, axis=0), moe_gain)
    normed_rows = lax.all_gather(picked, "ctx", axis=0, tiled=True)
    gate_val = jnp.dot(normed_rows, gate_weight[0], preferred_element_type=jnp.float32)
    up_val = jnp.dot(normed_rows, up_weight[0], preferred_element_type=jnp.float32)
    hidden = (jax.nn.silu(gate_val) * up_val).astype(jnp.bfloat16)
    sums_mine = lax.psum_scatter(
        jnp.dot(hidden, down_weight[0], preferred_element_type=jnp.float32).astype(jnp.bfloat16),
        "ctx",
        scatter_dimension=0,
        tiled=True,
    ).astype(jnp.float32)
    arrived = lax.all_to_all(
        sums_mine.astype(jnp.bfloat16), "exp", split_axis=1, concat_axis=0, tiled=True
    ).astype(sums_mine.dtype)
    piece_expert = jnp.arange(exp_count, dtype=jnp.int32) // split_count
    hit_expert = (expert_ids[:, :, None] == piece_expert[None, None, :]).astype(jnp.float32)
    hit_slot = (pick_rank[:, :, None] == jnp.arange(CAP, dtype=jnp.int32)[None, None, :]).astype(
        jnp.float32
    )
    combine_table = jnp.sum(
        route_weight[:, :, None, None] * hit_expert[:, :, :, None] * hit_slot[:, :, None, :], axis=1
    )
    combine_table = combine_table.reshape(tok_rows, exp_count * CAP)
    moe_slice = jnp.dot(
        combine_table, arrived, precision=lax.Precision.HIGHEST, preferred_element_type=jnp.float32
    )
    return (stream_slice.astype(jnp.float32) + moe_slice).astype(jnp.bfloat16)


def solution(mesh):
    placed = (
        P("ctx", None),
        P("ctx", "exp"),
        P("ctx", "exp"),
        P("ctx", None),
        P("ctx", None),
        P("exp", "ctx"),
        P("exp"),
        P("exp"),
        P("exp"),
        P("exp", "ctx"),
        P(),
        P("exp", None, "ctx"),
        P("exp", None, "ctx"),
        P("exp", "ctx", None),
        P("ctx", None),
        P("ctx", None),
    )
    return jax.shard_map(
        body, mesh=mesh, in_specs=placed, out_specs=P("ctx", "exp"), check_vma=False
    )
```

profile of v0, /device:TPU:0, one launch (start us, length us, event | category | flops | bytes accessed | tf_op | source)
XLA Modules:
  0.0 343.4 jit_solution(16639426668395161547)
XLA Ops:
  7.3 1.1 copy.60
  8.5 1.1 copy.61
  10.9 42.7 %while.11 = (s32[]{:T(128)}, f32[16,64,128]{2,1,0:T(8,128)S(1)}, f32[16,1]{0,1:T(1,128)S(1)}, f32[16,64,128]{2,1,0:T(8,128)S(1)}, s32[]{:T(128)}, /*index=5*/s32[]{:T(128)}) while((s32[]{:T(128)}, f32[16,64,128]{2,1,0:T(8,128)S(1)}, f32[16,1]{0,1:T(1,128)S(1)}, f32[16,64,128]{2,1,0:T(8,128)S(1)}, s32[]{:T(128)}, ...), condition=%wide.region_2.3_spmd.clone, body=%wide.region_1.2_spmd.clone.sunk | while | flops 655363 | bytes 3145911 | solution.py:106
  11.0 4.9 %collective-permute-start = (bf16[16,64,128]{2,1,0:T(8,128)(2,1)S(1)}, bf16[16,64,128]{2,1,0:T(8,128)(2,1)S(1)}, u32[]{:S(2)}, u32[]{:S(2)}) collective-permute-start(bf16[16,64,128]{2,1,0:T(8,128)(2,1)S(1)} %fusion.72), channel_id=1, source_target_pairs={{0,8},{8,16},{16,24},{1,9},{9,17},{17,25},{2,10},{10,18},{18,26},{... | collective-permute-start | bytes 786440 | tf_op jit(solution)/shard_map/while/body/eval_jaxpr/ppermute | solution.py:16
  15.9 5.5 %collective-permute-done = bf16[16,64,128]{2,1,0:T(8,128)(2,1)S(1)} collective-permute-done((bf16[16,64,128]{2,1,0:T(8,128)(2,1)S(1)}, bf16[16,64,128]{2,1,0:T(8,128)(2,1)S(1)}, u32[]{:S(2)}, u32[]{:S(2)}) %collective-permute-start) | collective-permute-done | bytes 262176 | tf_op jit(solution)/shard_map/while/body/eval_jaxpr/ppermute | solution.py:16
  21.6 4.4 %collective-permute-start = (bf16[16,64,128]{2,1,0:T(8,128)(2,1)S(1)}, bf16[16,64,128]{2,1,0:T(8,128)(2,1)S(1)}, u32[]{:S(2)}, u32[]{:S(2)}) collective-permute-start(bf16[16,64,128]{2,1,0:T(8,128)(2,1)S(1)} %fusion.72), channel_id=1, source_target_pairs={{0,8},{8,16},{16,24},{1,9},{9,17},{17,25},{2,10},{10,18},{18,26},{... | collective-permute-start | bytes 786440 | tf_op jit(solution)/shard_map/while/body/eval_jaxpr/ppermute | solution.py:16
  26.0 11.6 %collective-permute-done = bf16[16,64,128]{2,1,0:T(8,128)(2,1)S(1)} collective-permute-done((bf16[16,64,128]{2,1,0:T(8,128)(2,1)S(1)}, bf16[16,64,128]{2,1,0:T(8,128)(2,1)S(1)}, u32[]{:S(2)}, u32[]{:S(2)}) %collective-permute-start) | collective-permute-done | bytes 262176 | tf_op jit(solution)/shard_map/while/body/eval_jaxpr/ppermute | solution.py:16
  37.8 4.4 %collective-permute-start = (bf16[16,64,128]{2,1,0:T(8,128)(2,1)S(1)}, bf16[16,64,128]{2,1,0:T(8,128)(2,1)S(1)}, u32[]{:S(2)}, u32[]{:S(2)}) collective-permute-start(bf16[16,64,128]{2,1,0:T(8,128)(2,1)S(1)} %fusion.72), channel_id=1, source_target_pairs={{0,8},{8,16},{16,24},{1,9},{9,17},{17,25},{2,10},{10,18},{18,26},{... | collective-permute-start | bytes 786440 | tf_op jit(solution)/shard_map/while/body/eval_jaxpr/ppermute | solution.py:16
  42.2 11.3 %collective-permute-done = bf16[16,64,128]{2,1,0:T(8,128)(2,1)S(1)} collective-permute-done((bf16[16,64,128]{2,1,0:T(8,128)(2,1)S(1)}, bf16[16,64,128]{2,1,0:T(8,128)(2,1)S(1)}, u32[]{:S(2)}, u32[]{:S(2)}) %collective-permute-start) | collective-permute-done | bytes 262176 | tf_op jit(solution)/shard_map/while/body/eval_jaxpr/ppermute | solution.py:16
  56.1 54.2 %all-gather.4.cloned.1.call-done = bf16[1024,4096]{1,0:T(8,128)(2,1)} async-done(((bf16[1024,1024]{1,0:T(8,128)(2,1)}), bf16[1024,4096]{1,0:T(8,128)(2,1)}) %all-gather.4.cloned.1.call-update) | async-done | bytes 8388624 | tf_op jit(solution)/shard_map/all_gather | solution.py:123
  110.3 5.8 %convolution_convert_fusion = bf16[128,4096]{1,0:T(8,128)(2,1)} fusion(bf16[1024,4096]{1,0:T(8,128)(2,1)} %all-gather.4.cloned.1.call-done, f32[128,1024]{1,0:T(8,128)S(1)} %bitcast.99, f32[1024]{0:T(1024)S(1)} %copy-done.10, f32[128,1024]{1,0:T(8,128)S(1)} %copy.62, bf16[128,1024]{1,0:T(8,128)(2,1)S(1)} %copy-done.3), kind=kOutput, calls=%fused_computation.12 | convolution fusion | flops 1075445760 | bytes 10752000 | tf_op jit(solution)/shard_map/dot_general | solution.py:121
  116.2 58.9 %all-reduce.3.cloned.1.call-done = bf16[128,4096]{1,0:T(8,128)(2,1)} async-done(((bf16[128,4096]{1,0:T(8,128)(2,1)}), bf16[128,4096]{1,0:T(8,128)(2,1)}) %all-reduce.3.cloned.1.call-update) | async-done | bytes 1048592 | tf_op jit(solution)/shard_map/psum | solution.py:131
  175.1 1.7 add_convert_fusion
  177.8 20.3 %all-gather.6.cloned.1.call-done = bf16[128,4096]{1,0:T(8,128)(2,1)} async-done(((bf16[128,512]{1,0:T(8,128)(2,1)}), bf16[128,4096]{1,0:T(8,128)(2,1)}) %all-gather.6.cloned.1.call-update) | async-done | bytes 1048592 | tf_op jit(solution)/shard_map/all_gather | solution.py:135
  198.0 1.3 concatenate.3
  201.8 34.9 %all-gather.8.cloned.1.call-done = bf16[256,4096]{1,0:T(8,128)(2,1)} async-done(((bf16[64,4096]{1,0:T(8,128)(2,1)}), bf16[256,4096]{1,0:T(8,128)(2,1)}) %all-gather.8.cloned.1.call-update) | async-done | bytes 2097168 | tf_op jit(solution)/shard_map/all_gather | solution.py:141
  236.7 16.7 %fusion.6 = f32[256,3072]{1,0:T(8,128)} fusion(bf16[256,4096]{1,0:T(8,128)(2,1)} %all-gather.8.cloned.1.call-done, bf16[1,4096,3072]{2,1,0:T(8,128)(2,1)} %param.29), kind=kOutput, calls=%fused_computation.9 | convolution fusion | flops 6442450944 | bytes 30408704 | tf_op jit(solution)/shard_map/dot_general | solution.py:142
  253.4 25.1 %fusion.8 = bf16[256,4096]{1,0:T(8,128)(2,1)} fusion(bf16[1,3072,4096]{2,1,0:T(8,128)(2,1)} %param.31, bf16[256,4096]{1,0:T(8,128)(2,1)S(1)} %copy-done.9, bf16[1,4096,3072]{2,1,0:T(8,128)(2,1)} %param.30, f32[256,3072]{1,0:T(8,128)} %fusion.6), kind=kOutput, calls=%fused_computation.11 | convolution fusion | flops 12890669056 | bytes 57671680 | tf_op jit(solution)/shard_map/dot_general | solution.py:146
  278.5 35.4 %reduce-scatter.2.cloned.1.call-done = bf16[64,4096]{1,0:T(8,128)(2,1)} async-done(((bf16[256,4096]{1,0:T(8,128)(2,1)}), bf16[64,4096]{1,0:T(8,128)(2,1)}) %reduce-scatter.2.cloned.1.call-update) | async-done | bytes 524304 | tf_op jit(solution)/shard_map/reduce_scatter | solution.py:145
  313.9 1.9 copy.74
  315.8 4.6 %all-to-all-start = ((bf16[64,8,512]{2,0,1:T(8,128)(2,1)}), bf16[64,8,512]{2,0,1:T(8,128)(2,1)S(1)}, u32[]{:S(2)}, u32[]{:S(2)}) async-start(bf16[64,8,512]{2,0,1:T(8,128)(2,1)} %bitcast.90), calls=%async_computation.1 | async-start | bytes 1048576 | tf_op jit(solution)/shard_map/all_to_all | solution.py:151
  320.7 1.9 gather_fusion.1
  323.0 12.8 %all-to-all-done = bf16[64,8,512]{2,0,1:T(8,128)(2,1)S(1)} async-done(((bf16[64,8,512]{2,0,1:T(8,128)(2,1)}), bf16[64,8,512]{2,0,1:T(8,128)(2,1)S(1)}, u32[]{:S(2)}, u32[]{:S(2)}) %all-to-all-start) | async-done | bytes 524320 | tf_op jit(solution)/shard_map/all_to_all | solution.py:151
  335.8 1.1 fusion.31
  (87 shorter events, 8.9 us)
Async XLA Ops:
  6.5 47.1 %copy-start = (bf16[128,128]{1,0:T(8,128)(2,1)S(1)}, bf16[128,128]{1,0:T(8,128)(2,1)}, u32[]{:S(2)}) copy-start(bf16[128,128]{1,0:T(8,128)(2,1)} %param.22) | copy-start | bytes 98308
  6.5 3.0 copy-start.4
  6.5 3.0 copy-start.11
  6.5 3.1 copy-start.5
  6.5 103.8 %all-gather.4.cloned.1.call-start = ((), (), s32[]{:S(2)}) async-start(), calls=%async_computation.2 | async-start | bytes 10485760 | tf_op jit(solution)/shard_map/all_gather | solution.py:123
  7.3 167.9 %all-reduce.3.cloned.1.call-start = ((), (), s32[]{:S(2)}) async-start(), calls=%async_computation.3 | async-start | bytes 2097152 | tf_op jit(solution)/shard_map/psum | solution.py:131
  10.8 43.3 %copy-start.12 = (f32[16]{0:T(128)S(1)}, f32[16]{0:T(128)}, u32[]{:S(2)}) copy-start(f32[16]{0:T(128)} %param.25) | copy-start | bytes 196
  11.0 10.4 %collective-permute-start = (bf16[16,64,128]{2,1,0:T(8,128)(2,1)S(1)}, bf16[16,64,128]{2,1,0:T(8,128)(2,1)S(1)}, u32[]{:S(2)}, u32[]{:S(2)}) collective-permute-start(bf16[16,64,128]{2,1,0:T(8,128)(2,1)S(1)} %fusion.72), channel_id=1, source_target_pairs={{0,8},{8,16},{16,24},{1,9},{9,17},{17,25},{2,10},{10,18},{18,26},{... | collective-permute-start | bytes 786440 | tf_op jit(solution)/shard_map/while/body/eval_jaxpr/ppermute | solution.py:16
  21.6 16.0 %collective-permute-start = (bf16[16,64,128]{2,1,0:T(8,128)(2,1)S(1)}, bf16[16,64,128]{2,1,0:T(8,128)(2,1)S(1)}, u32[]{:S(2)}, u32[]{:S(2)}) collective-permute-start(bf16[16,64,128]{2,1,0:T(8,128)(2,1)S(1)} %fusion.72), channel_id=1, source_target_pairs={{0,8},{8,16},{16,24},{1,9},{9,17},{17,25},{2,10},{10,18},{18,26},{... | collective-permute-start | bytes 786440 | tf_op jit(solution)/shard_map/while/body/eval_jaxpr/ppermute | solution.py:16
  37.8 15.7 %collective-permute-start = (bf16[16,64,128]{2,1,0:T(8,128)(2,1)S(1)}, bf16[16,64,128]{2,1,0:T(8,128)(2,1)S(1)}, u32[]{:S(2)}, u32[]{:S(2)}) collective-permute-start(bf16[16,64,128]{2,1,0:T(8,128)(2,1)S(1)} %fusion.72), channel_id=1, source_target_pairs={{0,8},{8,16},{16,24},{1,9},{9,17},{17,25},{2,10},{10,18},{18,26},{... | collective-permute-start | bytes 786440 | tf_op jit(solution)/shard_map/while/body/eval_jaxpr/ppermute | solution.py:16
  53.6 1.3 copy-start.3
  54.7 55.6 %copy-start.10 = (f32[1024]{0:T(1024)S(1)}, f32[1024]{0:T(1024)}, u32[]{:S(2)}) copy-start(f32[1024]{0:T(1024)} %param.26) | copy-start | bytes 12292
  110.3 66.5 %copy-start.7 = (s32[128,2]{0,1:T(2,128)S(1)}, s32[128,2]{0,1:T(2,128)}, u32[]{:S(2)}) copy-start(s32[128,2]{0,1:T(2,128)} %param.32) | copy-start | bytes 3076
  116.2 81.8 %all-gather.6.cloned.1.call-start = ((), (), s32[]{:S(2)}) async-start(), calls=%async_computation.4 | async-start | bytes 1179648 | tf_op jit(solution)/shard_map/all_gather | solution.py:135
  176.8 59.9 %all-gather.8.cloned.1.call-start = ((), (), s32[]{:S(2)}) async-start(), calls=%async_computation.5 | async-start | bytes 2621440 | tf_op jit(solution)/shard_map/all_gather | solution.py:141
  199.4 1.2 copy-start.6
  201.6 112.3 %reduce-scatter.2.cloned.1.call-start = ((), (), s32[]{:S(2)}) async-start(), calls=%async_computation.6 | async-start | bytes 2621440 | tf_op jit(solution)/shard_map/reduce_scatter | solution.py:145
  236.7 16.7 %copy-start.9 = (bf16[256,4096]{1,0:T(8,128)(2,1)S(1)}, bf16[256,4096]{1,0:T(8,128)(2,1)}, u32[]{:S(2)}) copy-start(bf16[256,4096]{1,0:T(8,128)(2,1)} %all-gather.8.cloned.1.call-done) | copy-start | bytes 6291460
  315.8 20.0 %all-to-all-start = ((bf16[64,8,512]{2,0,1:T(8,128)(2,1)}), bf16[64,8,512]{2,0,1:T(8,128)(2,1)S(1)}, u32[]{:S(2)}, u32[]{:S(2)}) async-start(bf16[64,8,512]{2,0,1:T(8,128)(2,1)} %bitcast.90), calls=%async_computation.1 | async-start | bytes 1048576 | tf_op jit(solution)/shard_map/all_to_all | solution.py:151
  320.7 2.2 copy-start.8
  320.7 15.1 %copy-start.2 = (bf16[128,512]{1,0:T(8,128)(2,1)S(1)}, bf16[128,512]{1,0:T(8,128)(2,1)}, u32[]{:S(2)}) copy-start(bf16[128,512]{1,0:T(8,128)(2,1)} %add_convert_fusion) | copy-start | bytes 393220
  320.7 16.2 %copy-start.1 = (bf16[128,128]{1,0:T(8,128)(2,1)S(1)}, bf16[128,128]{1,0:T(8,128)(2,1)}, u32[]{:S(2)}) copy-start(bf16[128,128]{1,0:T(8,128)(2,1)} %param.22) | copy-start | bytes 98308
Sparse Core Ops, SparseCore 0:
  9.2 101.0 all-gather.3
  116.3 58.7 all-reduce.2
  176.9 21.0 all-gather.5
  201.7 34.9 all-gather.7
  278.7 35.1 reduce-scatter.1
where the time goes:
time: 344 us; the launch traced here: 343 us
  waiting for transfers between devices  246 us (72%)
  matrix products  50.4 us (15%)
  starting transfers between devices  18.6 us (5%)
  between operations  13.5 us (4%)
  local copies, waits for them, and re-layouts  9.85 us (3%)
  other arithmetic  5.34 us (2%)
    psum x1, waiting for transfers between devices, body(): lax.psum(ssm_terms.astype(jnp.bfloat16), 'exp').astype(jnp.float32)  58.9 us
    all_gather x1, waiting for transfers between devices, body(): lax.all_gather(out_weight, 'ctx', axis=1, tiled=True)  54.2 us
    reduce_scatter x1, waiting for transfers between devices, body(): lax.psum_scatter(jnp.dot(hidden, down_weight[0], preferred_element_type=j...  35.4 us
    all_gather x1, waiting for transfers between devices, body(): normed_rows = lax.all_gather(picked, 'ctx', axis=0, tiled=True)  34.9 us
    ppermute x3, waiting for transfers between devices, passed_along(): return lax.ppermute(block, axis, route)  28.4 us
    dot_general x1, matrix products, body(): jnp.dot(hidden, down_weight[0], preferred_element_type=jnp.float32)  25.1 us
    all_gather x1, waiting for transfers between devices, body(): stream_full = lax.all_gather(stream_slice, 'exp', axis=1, tiled=True)  20.3 us
    dot_general x1, matrix products, body(): jnp.dot(normed_rows, gate_weight[0], preferred_element_type=jnp.float32)  16.7 us
  transfers between devices with their start and end apart: 9, of which 9 were waited for; matrix products, arithmetic and copies ran while one was open for 3% of the time, Pallas kernels for 0%

commit v1 on v0

--- a/solution.py
+++ b/solution.py
@@ -8,6 +8,10 @@
 EXPERTS = 8
 CAP = 64
 EPSILON = 1e-05
+
+
+def part_local_data(array_in, bus_axis):
+    return lax.all_gather(array_in, bus_axis).sum(axis=0)
 
 
 def passed_along(block, axis, distance):
@@ -128,7 +132,7 @@
     slice_width = residual.shape[1] // exp_count
     split_count = exp_count // EXPERTS
     own_residual = lax.dynamic_slice_in_dim(residual, exp_index * slice_width, slice_width, 1)
-    ssm_sum = lax.psum(ssm_terms.astype(jnp.bfloat16), "exp").astype(jnp.float32)
+    ssm_sum = part_local_data(ssm_terms.astype(jnp.bfloat16), "exp").astype(jnp.float32)
     ssm_share = lax.dynamic_slice_in_dim(ssm_sum, exp_index * slice_width, slice_width, 1)
     stream_slice = (own_residual.astype(jnp.float32) + ssm_share).astype(jnp.bfloat16)
     token_of_slot, pick_rank = slot_tables(expert_ids)

time: 344 us -> 372 us (1.081)
  waiting for transfers between devices: 246 us -> 268 us
  other arithmetic: 5.34 us -> 10.2 us
    all_gather x0 -> x1, waiting for transfers between devices: none -> 82.2 us  [part_local_data(): return lax.all_gather(array_in, bus_axis).sum(axis=0)]
    psum x1 -> x0, waiting for transfers between devices: 58.9 us -> none  [body(): lax.psum(ssm_terms.astype(jnp.bfloat16), 'exp').astype(jnp.float32)]
    reduce_sum x0 -> x1, other arithmetic: none -> 4.91 us  [part_local_data(): return lax.all_gather(array_in, bus_axis).sum(axis=0)]
where the time goes in v1:
time: 372 us; the launch traced here: 371 us
  waiting for transfers between devices  268 us (72%)
  matrix products  50.5 us (14%)
  starting transfers between devices  18.6 us (5%)
  between operations  13.5 us (4%)
  other arithmetic  10.2 us (3%)
  local copies, waits for them, and re-layouts  9.85 us (3%)
    all_gather x1, waiting for transfers between devices, part_local_data(): return lax.all_gather(array_in, bus_axis).sum(axis=0)  82.2 us
    all_gather x1, waiting for transfers between devices, body(): lax.all_gather(out_weight, 'ctx', axis=1, tiled=True)  54.2 us
    reduce_scatter x1, waiting for transfers between devices, body(): lax.psum_scatter(jnp.dot(hidden, down_weight[0], preferred_element_type=j...  35.4 us
    all_gather x1, waiting for transfers between devices, body(): normed_rows = lax.all_gather(picked, 'ctx', axis=0, tiled=True)  34.9 us
    ppermute x3, waiting for transfers between devices, passed_along(): return lax.ppermute(block, axis, route)  28.4 us
    dot_general x1, matrix products, body(): jnp.dot(hidden, down_weight[0], preferred_element_type=jnp.float32)  25.2 us
    all_gather x1, waiting for transfers between devices, body(): stream_full = lax.all_gather(stream_slice, 'exp', axis=1, tiled=True)  19.8 us
    dot_general x1, matrix products, body(): jnp.dot(normed_rows, gate_weight[0], preferred_element_type=jnp.float32)  16.7 us
  transfers between devices with their start and end apart: 9, of which 9 were waited for; matrix products, arithmetic and copies ran while one was open for 3% of the time, Pallas kernels for 0%

profile of v1, /device:TPU:0, one launch (start us, length us, event | category | flops | bytes accessed | tf_op | source)
XLA Modules:
  0.0 371.2 jit_solution(3621426297183494393)
XLA Ops:
  7.3 1.1 copy.60
  10.9 42.7 %while.11 = (s32[]{:T(128)}, f32[16,64,128]{2,1,0:T(8,128)S(1)}, f32[16,1]{0,1:T(1,128)S(1)}, f32[16,64,128]{2,1,0:T(8,128)S(1)}, s32[]{:T(128)}, /*index=5*/s32[]{:T(128)}) while((s32[]{:T(128)}, f32[16,64,128]{2,1,0:T(8,128)S(1)}, f32[16,1]{0,1:T(1,128)S(1)}, f32[16,64,128]{2,1,0:T(8,128)S(1)}, s32[]{:T(128)}, ...), condition=%wide.region_2.3_spmd.clone, body=%wide.region_1.2_spmd.clone.sunk | while | flops 655363 | bytes 3145911 | solution.py:110
  11.0 4.9 %collective-permute-start = (bf16[16,64,128]{2,1,0:T(8,128)(2,1)S(1)}, bf16[16,64,128]{2,1,0:T(8,128)(2,1)S(1)}, u32[]{:S(2)}, u32[]{:S(2)}) collective-permute-start(bf16[16,64,128]{2,1,0:T(8,128)(2,1)S(1)} %fusion.72), channel_id=1, source_target_pairs={{0,8},{8,16},{16,24},{1,9},{9,17},{17,25},{2,10},{10,18},{18,26},{... | collective-permute-start | bytes 786440 | tf_op jit(solution)/shard_map/while/body/eval_jaxpr/ppermute | solution.py:20
  15.9 5.5 %collective-permute-done = bf16[16,64,128]{2,1,0:T(8,128)(2,1)S(1)} collective-permute-done((bf16[16,64,128]{2,1,0:T(8,128)(2,1)S(1)}, bf16[16,64,128]{2,1,0:T(8,128)(2,1)S(1)}, u32[]{:S(2)}, u32[]{:S(2)}) %collective-permute-start) | collective-permute-done | bytes 262176 | tf_op jit(solution)/shard_map/while/body/eval_jaxpr/ppermute | solution.py:20
  21.6 4.4 %collective-permute-start = (bf16[16,64,128]{2,1,0:T(8,128)(2,1)S(1)}, bf16[16,64,128]{2,1,0:T(8,128)(2,1)S(1)}, u32[]{:S(2)}, u32[]{:S(2)}) collective-permute-start(bf16[16,64,128]{2,1,0:T(8,128)(2,1)S(1)} %fusion.72), channel_id=1, source_target_pairs={{0,8},{8,16},{16,24},{1,9},{9,17},{17,25},{2,10},{10,18},{18,26},{... | collective-permute-start | bytes 786440 | tf_op jit(solution)/shard_map/while/body/eval_jaxpr/ppermute | solution.py:20
  26.0 11.6 %collective-permute-done = bf16[16,64,128]{2,1,0:T(8,128)(2,1)S(1)} collective-permute-done((bf16[16,64,128]{2,1,0:T(8,128)(2,1)S(1)}, bf16[16,64,128]{2,1,0:T(8,128)(2,1)S(1)}, u32[]{:S(2)}, u32[]{:S(2)}) %collective-permute-start) | collective-permute-done | bytes 262176 | tf_op jit(solution)/shard_map/while/body/eval_jaxpr/ppermute | solution.py:20
  37.8 4.4 %collective-permute-start = (bf16[16,64,128]{2,1,0:T(8,128)(2,1)S(1)}, bf16[16,64,128]{2,1,0:T(8,128)(2,1)S(1)}, u32[]{:S(2)}, u32[]{:S(2)}) collective-permute-start(bf16[16,64,128]{2,1,0:T(8,128)(2,1)S(1)} %fusion.72), channel_id=1, source_target_pairs={{0,8},{8,16},{16,24},{1,9},{9,17},{17,25},{2,10},{10,18},{18,26},{... | collective-permute-start | bytes 786440 | tf_op jit(solution)/shard_map/while/body/eval_jaxpr/ppermute | solution.py:20
  42.2 11.3 %collective-permute-done = bf16[16,64,128]{2,1,0:T(8,128)(2,1)S(1)} collective-permute-done((bf16[16,64,128]{2,1,0:T(8,128)(2,1)S(1)}, bf16[16,64,128]{2,1,0:T(8,128)(2,1)S(1)}, u32[]{:S(2)}, u32[]{:S(2)}) %collective-permute-start) | collective-permute-done | bytes 262176 | tf_op jit(solution)/shard_map/while/body/eval_jaxpr/ppermute | solution.py:20
  56.1 54.2 %all-gather.6.cloned.1.call-done = bf16[1024,4096]{1,0:T(8,128)(2,1)} async-done(((bf16[1024,1024]{1,0:T(8,128)(2,1)}), bf16[1024,4096]{1,0:T(8,128)(2,1)}) %all-gather.6.cloned.1.call-update) | async-done | bytes 8388624 | tf_op jit(solution)/shard_map/all_gather | solution.py:127
  110.3 5.8 %convolution_convert_fusion = bf16[128,4096]{1,0:T(8,128)(2,1)} fusion(bf16[1024,4096]{1,0:T(8,128)(2,1)} %all-gather.6.cloned.1.call-done, f32[128,1024]{1,0:T(8,128)S(1)} %bitcast.101, f32[1024]{0:T(1024)S(1)} %copy-done.10, f32[128,1024]{1,0:T(8,128)S(1)} %copy.62, bf16[128,1024]{1,0:T(8,128)(2,1)S(1)} %copy-done.3), kind=kOutput, calls=%fused_computation.12 | convolution fusion | flops 1075445760 | bytes 10752000 | tf_op jit(solution)/shard_map/dot_general | solution.py:125
  116.2 82.2 %all-gather.12.cloned.1.call-done = bf16[1024,4096]{1,0:T(8,128)(2,1)} async-done(((bf16[128,4096]{1,0:T(8,128)(2,1)}), bf16[1024,4096]{1,0:T(8,128)(2,1)}) %all-gather.12.cloned.1.call-update) | async-done | bytes 8388624 | tf_op jit(solution)/shard_map/all_gather | solution.py:14
  198.4 4.9 %reduce_sum.58 = bf16[128,4096]{1,0:T(8,128)(2,1)S(1)} reduce(bf16[8,128,4096]{2,1,0:T(8,128)(2,1)} %bitcast.94, bf16[]{:T(256)} %constant.94.clone.1), dimensions={0}, to_apply=%region_4.5 | reduce | flops 3670016 | bytes 9437186 | tf_op jit(solution)/shard_map/reduce_sum | solution.py:14
  203.3 1.6 add_convert_fusion
  205.9 19.8 %all-gather.8.cloned.1.call-done = bf16[128,4096]{1,0:T(8,128)(2,1)} async-done(((bf16[128,512]{1,0:T(8,128)(2,1)}), bf16[128,4096]{1,0:T(8,128)(2,1)}) %all-gather.8.cloned.1.call-update) | async-done | bytes 1048592 | tf_op jit(solution)/shard_map/all_gather | solution.py:139
  225.7 1.3 concatenate.3
  229.5 34.9 %all-gather.10.cloned.1.call-done = bf16[256,4096]{1,0:T(8,128)(2,1)} async-done(((bf16[64,4096]{1,0:T(8,128)(2,1)}), bf16[256,4096]{1,0:T(8,128)(2,1)}) %all-gather.10.cloned.1.call-update) | async-done | bytes 2097168 | tf_op jit(solution)/shard_map/all_gather | solution.py:145
  264.4 16.7 %fusion.6 = f32[256,3072]{1,0:T(8,128)} fusion(bf16[256,4096]{1,0:T(8,128)(2,1)} %all-gather.10.cloned.1.call-done, bf16[1,4096,3072]{2,1,0:T(8,128)(2,1)} %param.29), kind=kOutput, calls=%fused_computation.9 | convolution fusion | flops 6442450944 | bytes 30408704 | tf_op jit(solution)/shard_map/dot_general | solution.py:146
  281.1 25.2 %fusion.8 = bf16[256,4096]{1,0:T(8,128)(2,1)} fusion(bf16[1,3072,4096]{2,1,0:T(8,128)(2,1)} %param.31, bf16[256,4096]{1,0:T(8,128)(2,1)S(1)} %copy-done.9, bf16[1,4096,3072]{2,1,0:T(8,128)(2,1)} %param.30, f32[256,3072]{1,0:T(8,128)} %fusion.6), kind=kOutput, calls=%fused_computation.11 | convolution fusion | flops 12890669056 | bytes 57671680 | tf_op jit(solution)/shard_map/dot_general | solution.py:150
  306.3 35.4 %reduce-scatter.2.cloned.1.call-done = bf16[64,4096]{1,0:T(8,128)(2,1)} async-done(((bf16[256,4096]{1,0:T(8,128)(2,1)}), bf16[64,4096]{1,0:T(8,128)(2,1)}) %reduce-scatter.2.cloned.1.call-update) | async-done | bytes 524304 | tf_op jit(solution)/shard_map/reduce_scatter | solution.py:149
  341.7 1.9 copy.74
  343.6 4.6 %all-to-all-start = ((bf16[64,8,512]{2,0,1:T(8,128)(2,1)}), bf16[64,8,512]{2,0,1:T(8,128)(2,1)S(1)}, u32[]{:S(2)}, u32[]{:S(2)}) async-start(bf16[64,8,512]{2,0,1:T(8,128)(2,1)} %bitcast.91), calls=%async_computation.1 | async-start | bytes 1048576 | tf_op jit(solution)/shard_map/all_to_all | solution.py:155
  348.5 1.9 gather_fusion.1
  350.8 12.8 %all-to-all-done = bf16[64,8,512]{2,0,1:T(8,128)(2,1)S(1)} async-done(((bf16[64,8,512]{2,0,1:T(8,128)(2,1)}), bf16[64,8,512]{2,0,1:T(8,128)(2,1)S(1)}, u32[]{:S(2)}, u32[]{:S(2)}) %all-to-all-start) | async-done | bytes 524320 | tf_op jit(solution)/shard_map/all_to_all | solution.py:155
  363.6 1.1 fusion.31
  (88 shorter events, 10.0 us)
Async XLA Ops:
  6.5 47.1 %copy-start = (bf16[128,128]{1,0:T(8,128)(2,1)S(1)}, bf16[128,128]{1,0:T(8,128)(2,1)}, u32[]{:S(2)}) copy-start(bf16[128,128]{1,0:T(8,128)(2,1)} %param.22) | copy-start | bytes 98308
  6.5 3.0 copy-start.4
  6.5 3.0 copy-start.11
  6.5 3.1 copy-start.5
  6.5 103.8 %all-gather.6.cloned.1.call-start = ((), (), s32[]{:S(2)}) async-start(), calls=%async_computation.2 | async-start | bytes 10485760 | tf_op jit(solution)/shard_map/all_gather | solution.py:127
  7.3 191.1 %all-gather.12.cloned.1.call-start = ((), (), s32[]{:S(2)}) async-start(), calls=%async_computation.6 | async-start | bytes 9437184 | tf_op jit(solution)/shard_map/all_gather | solution.py:14
  10.8 43.3 %copy-start.12 = (f32[16]{0:T(128)S(1)}, f32[16]{0:T(128)}, u32[]{:S(2)}) copy-start(f32[16]{0:T(128)} %param.25) | copy-start | bytes 196
  11.0 10.4 %collective-permute-start = (bf16[16,64,128]{2,1,0:T(8,128)(2,1)S(1)}, bf16[16,64,128]{2,1,0:T(8,128)(2,1)S(1)}, u32[]{:S(2)}, u32[]{:S(2)}) collective-permute-start(bf16[16,64,128]{2,1,0:T(8,128)(2,1)S(1)} %fusion.72), channel_id=1, source_target_pairs={{0,8},{8,16},{16,24},{1,9},{9,17},{17,25},{2,10},{10,18},{18,26},{... | collective-permute-start | bytes 786440 | tf_op jit(solution)/shard_map/while/body/eval_jaxpr/ppermute | solution.py:20
  21.6 16.0 %collective-permute-start = (bf16[16,64,128]{2,1,0:T(8,128)(2,1)S(1)}, bf16[16,64,128]{2,1,0:T(8,128)(2,1)S(1)}, u32[]{:S(2)}, u32[]{:S(2)}) collective-permute-start(bf16[16,64,128]{2,1,0:T(8,128)(2,1)S(1)} %fusion.72), channel_id=1, source_target_pairs={{0,8},{8,16},{16,24},{1,9},{9,17},{17,25},{2,10},{10,18},{18,26},{... | collective-permute-start | bytes 786440 | tf_op jit(solution)/shard_map/while/body/eval_jaxpr/ppermute | solution.py:20
  37.8 15.7 %collective-permute-start = (bf16[16,64,128]{2,1,0:T(8,128)(2,1)S(1)}, bf16[16,64,128]{2,1,0:T(8,128)(2,1)S(1)}, u32[]{:S(2)}, u32[]{:S(2)}) collective-permute-start(bf16[16,64,128]{2,1,0:T(8,128)(2,1)S(1)} %fusion.72), channel_id=1, source_target_pairs={{0,8},{8,16},{16,24},{1,9},{9,17},{17,25},{2,10},{10,18},{18,26},{... | collective-permute-start | bytes 786440 | tf_op jit(solution)/shard_map/while/body/eval_jaxpr/ppermute | solution.py:20
  53.6 1.3 copy-start.3
  54.7 55.6 %copy-start.10 = (f32[1024]{0:T(1024)S(1)}, f32[1024]{0:T(1024)}, u32[]{:S(2)}) copy-start(f32[1024]{0:T(1024)} %param.26) | copy-start | bytes 12292
  116.2 109.6 %all-gather.8.cloned.1.call-start = ((), (), s32[]{:S(2)}) async-start(), calls=%async_computation.3 | async-start | bytes 1179648 | tf_op jit(solution)/shard_map/all_gather | solution.py:139
  198.4 6.6 %copy-start.7 = (s32[128,2]{0,1:T(2,128)S(1)}, s32[128,2]{0,1:T(2,128)}, u32[]{:S(2)}) copy-start(s32[128,2]{0,1:T(2,128)} %param.32) | copy-start | bytes 3076
  204.9 59.5 %all-gather.10.cloned.1.call-start = ((), (), s32[]{:S(2)}) async-start(), calls=%async_computation.4 | async-start | bytes 2621440 | tf_op jit(solution)/shard_map/all_gather | solution.py:145
  227.0 1.2 copy-start.6
  229.3 112.4 %reduce-scatter.2.cloned.1.call-start = ((), (), s32[]{:S(2)}) async-start(), calls=%async_computation.5 | async-start | bytes 2621440 | tf_op jit(solution)/shard_map/reduce_scatter | solution.py:149
  264.4 16.7 %copy-start.9 = (bf16[256,4096]{1,0:T(8,128)(2,1)S(1)}, bf16[256,4096]{1,0:T(8,128)(2,1)}, u32[]{:S(2)}) copy-start(bf16[256,4096]{1,0:T(8,128)(2,1)} %all-gather.10.cloned.1.call-done) | copy-start | bytes 6291460
  343.6 20.0 %all-to-all-start = ((bf16[64,8,512]{2,0,1:T(8,128)(2,1)}), bf16[64,8,512]{2,0,1:T(8,128)(2,1)S(1)}, u32[]{:S(2)}, u32[]{:S(2)}) async-start(bf16[64,8,512]{2,0,1:T(8,128)(2,1)} %bitcast.91), calls=%async_computation.1 | async-start | bytes 1048576 | tf_op jit(solution)/shard_map/all_to_all | solution.py:155
  348.5 2.2 copy-start.8
  348.5 15.1 %copy-start.2 = (bf16[128,512]{1,0:T(8,128)(2,1)S(1)}, bf16[128,512]{1,0:T(8,128)(2,1)}, u32[]{:S(2)}) copy-start(bf16[128,512]{1,0:T(8,128)(2,1)} %add_convert_fusion) | copy-start | bytes 393220
  348.5 16.2 %copy-start.1 = (bf16[128,128]{1,0:T(8,128)(2,1)S(1)}, bf16[128,128]{1,0:T(8,128)(2,1)}, u32[]{:S(2)}) copy-start(bf16[128,128]{1,0:T(8,128)(2,1)} %param.22) | copy-start | bytes 98308
Sparse Core Ops, SparseCore 0:
  9.2 101.0 all-gather.5
  116.3 82.0 all-gather.11
  205.0 20.6 all-gather.7
  229.4 34.9 all-gather.9
  306.5 35.1 reduce-scatter.1
